TPU v7x, 512 devices: a whole 4x4x16 slice. The times are simulated.
512 devices in a mesh: grid: 64 (over z, y_hi, core), orb: 8 (over y_lo, x).
Axes of the slice: x: 4, y: 4 (y_hi: 2, y_lo: 2; y = y_hi * 2 + y_lo), z: 16, core: 2. Of those that a mesh axis runs over, the one named last changes fastest.
Arguments:
- orbitals: bfloat16 [16384, 8192], P('grid', 'orb'), may hold values from -6 to 6
- points: int32 [4096], P('grid'), may hold values from 0 to 16383, as said below
Outputs:
- fitted: float32 [16384, 4096], P('grid', 'orb')
- gram: float32 [4096, 4096], P('grid', 'orb')
- density: float32 [4096], P('grid')
Inputs may be any that keep to these rules, and one draw needn't show every extreme that they name: `points`: entries 64 * g to 64 * g + 63 are distinct grid rows of slab g, the rows 256 * g to 256 * g + 255.
All inputs are finite; a program needn't handle non-finite values.
Results may differ from a plain program's by a relative error of at most 0.0003.
Values may be sent and summed in bfloat16 or wider, within the bound.
No kernel may reach another device: no remote copies, remote signals or barrier semaphores. Data moves between devices by JAX's collectives and lax.ppermute only.
A program may use at most 64 MiB of HBM per device.

v0:
```python
import jax
import jax.numpy as jnp
from jax import lax
from jax.sharding import Mesh
from jax.sharding import PartitionSpec as P

NORB = 8192
GRID = ("grid_0", "grid_1", "grid_2")


def joined_along(pieces, dim):
    pieces = jnp.moveaxis(pieces, 0, dim)
    shape = pieces.shape
    return pieces.reshape(*shape[:dim], shape[dim] * shape[dim + 1], *shape[dim + 2 :])


def all_blocks(value, axes, turns):
    pieces = value[None]
    for k in turns:
        pieces = lax.all_gather(pieces, axes[k], axis=0, tiled=True)
    current = [lax.axis_size(axes[k]) for k in reversed(turns)]
    pieces = pieces.reshape(*current, *value.shape)
    turned = sorted(range(len(turns)), key=lambda place: turns[len(turns) - 1 - place])
    return pieces.transpose(*turned, *range(len(turns), pieces.ndim)).reshape(-1, *value.shape)


def whole_of(value, axes, turns, dim):
    return joined_along(all_blocks(value, axes, turns), dim)


def side_by_side(arrays, axis, dim, along):
    widths = [a.shape[along] for a in arrays]
    both = jnp.concatenate(arrays, axis=along)
    whole = lax.psum_scatter(both, axis, scatter_dimension=dim, tiled=True)
    return tuple(jnp.split(whole, [sum(widths[:k]) for k in range(1, len(widths))], axis=along))


def sent_to_all(value, axis):
    copies = jnp.broadcast_to(value, (lax.axis_size(axis), *value.shape))
    return lax.all_to_all(copies, axis, split_axis=0, concat_axis=0, tiled=True)


def over_copies(value, axis):
    return sent_to_all(value, axis).sum(axis=0)


def contract(left, right):
    return lax.dot_general(
        left, right, (((1,), (1,)), ((), ())), preferred_element_type=jnp.float32
    )


def on_device(orbitals, points):
    rows = orbitals.shape[0]
    mu_dev = points.shape[0]
    total_mu = mu_dev * lax.axis_size(GRID)
    slab_start = lax.axis_index(GRID) * rows
    local_rows = points - slab_start
    chosen = jnp.take(orbitals, local_rows, axis=0)
    chosen_wide = chosen.astype(jnp.float32)
    dens_part = jnp.sum(chosen_wide * chosen_wide, axis=1)
    every = whole_of(chosen, GRID, (1, 0, 2), 0)
    pair = contract(orbitals, every)
    correlation = contract(chosen, every)
    width = total_mu // lax.axis_size("orb")
    col_start = lax.axis_index("orb") * width
    pair_share, over_share = side_by_side((pair, correlation), "orb", 1, 0)
    dens_all = over_copies(dens_part, "orb")
    scale = 1.0 / jnp.sqrt(jnp.float32(NORB))
    fitted = jnp.square(pair_share * scale)
    row_ids = lax.axis_index(GRID) * mu_dev + jnp.arange(mu_dev, dtype=jnp.int32)
    col_ids = col_start + jnp.arange(width, dtype=jnp.int32)
    diagonal_mask = row_ids[:, None] == col_ids[None, :]
    gram = jnp.where(diagonal_mask, jnp.float32(0.0), jnp.square(over_share * scale))
    density = dens_all / jnp.float32(NORB)
    return (fitted, gram, density)


def solution(mesh):
    torus = Mesh(
        mesh.devices.reshape(16, 2, 2, mesh.shape["orb"]), ("grid_0", "grid_1", "grid_2", "orb")
    )
    in_specs = (P(GRID, "orb"), P(GRID))
    out_specs = (P(GRID, "orb"), P(GRID, "orb"), P(GRID))
    return jax.shard_map(
        on_device, mesh=torus, in_specs=in_specs, out_specs=out_specs, check_vma=False
    )
```

profile of v0, /device:TPU:1, one launch (start us, length us, event | category | flops | bytes accessed | tf_op | source)
XLA Modules:
  0.0 230.9 jit_solution(3871971614468897059)
XLA Ops:
  7.2 0.0 copy-start
  7.2 0.0 all-gather.3.cloned.1.call-start
  7.2 0.7 compare_and_fusion
  8.0 0.3 copy-done
  8.2 0.7 gather_fusion
  8.9 0.1 bitcast_select_fusion
  9.0 6.8 %all_gather.9 = bf16[2,64,1024]{2,1,0:T(8,128)(2,1)} all-gather(bf16[1,64,1024]{2,1,0:T(8,128)(2,1)S(1)} %bitcast_select_fusion), channel_id=1, replica_groups=mesh['grid_0'=16,'grid_1'=2,'grid_2'=2,'orb'=8] {'grid_1'}, dimensions={0}, use_global_device_ids=true | all-gather | bytes 393216 | tf_op jit(solution)/shard_map/all_gather | solution.py:20
  15.9 0.0 all-gather.3.cloned.1.call-update
  15.9 0.0 all-gather.5.cloned.1.call-start
  15.9 75.3 %all-gather.3.cloned.1.call-done = bf16[32,64,1024]{2,1,0:T(8,128)(2,1)} async-done(((bf16[2,64,1024]{2,1,0:T(8,128)(2,1)}), bf16[32,64,1024]{2,1,0:T(8,128)(2,1)}) %all-gather.3.cloned.1.call-update) | async-done | bytes 4194320 | tf_op jit(solution)/shard_map/all_gather | solution.py:20
  91.2 0.0 all-gather.5.cloned.1.call-update
  91.3 0.0 reduce-scatter.2.cloned.1.call-start
  91.3 39.0 %all-gather.5.cloned.1.call-done = bf16[64,64,1024]{2,1,0:T(8,128)(2,1)} async-done(((bf16[32,64,1024]{2,1,0:T(8,128)(2,1)}), bf16[64,64,1024]{2,1,0:T(8,128)(2,1)}) %all-gather.5.cloned.1.call-update) | async-done | bytes 8388624 | tf_op jit(solution)/shard_map/all_gather | solution.py:20
  130.3 8.4 %copy.8 = bf16[16,2,2,64,1024]{4,3,2,1,0:T(8,128)(2,1)} copy(bf16[16,2,2,64,1024]{4,3,1,0,2:T(8,128)(2,1)} %bitcast.14) | data formatting | bytes 16777216 | tf_op jit(solution)/shard_map/transpose | solution.py:24
  138.7 0.0 copy-start.1
  138.7 6.2 %fusion.3 = f32[64,4096]{1,0:T(8,128)S(1)} fusion(bf16[4096,1024]{1,0:T(8,128)(2,1)} %bitcast.12, bf16[64,1024]{1,0:T(8,128)(2,1)S(1)} %gather_fusion, pred[64]{0:T(512)(128)(4,1)S(1)} %get-tuple-element.3), kind=kOutput, calls=%fused_computation.11 | convolution fusion | flops 536936448 | bytes 9568320 | tf_op jit(solution)/shard_map/dot_general | solution.py:48
  144.9 0.0 copy-done.1
  144.9 2.4 %convolution_bitcast_fusion = f32[256,4096]{1,0:T(8,128)S(1)} fusion(bf16[4096,1024]{1,0:T(8,128)(2,1)S(1)} %bitcast.13, bf16[256,1024]{1,0:T(8,128)(2,1)S(1)} %copy-done), kind=kOutput, calls=%fused_computation.1 | convolution fusion | flops 2147483648 | bytes 13107200 | tf_op jit(solution)/shard_map/dot_general | solution.py:48
  147.3 2.9 %pad_maximum_fusion = f32[320,4096]{1,0:T(8,128)} fusion(f32[64,4096]{1,0:T(8,128)S(1)} %fusion.3, f32[256,4096]{1,0:T(8,128)S(1)} %convolution_bitcast_fusion), kind=kLoop, calls=%fused_computation.2 | loop fusion | flops 1310720 | bytes 10485760 | tf_op jit(solution)/shard_map/concatenate | solution.py:33
  150.2 0.0 reduce-scatter.2.cloned.1.call-update
  150.2 0.2 multiply_reduce_fusion
  150.4 0.6 broadcast_in_dim.32
  151.0 3.9 %all-to-all-start = ((f32[8,1,64]{2,1,0:T(1,128)}), f32[8,1,64]{2,1,0:T(1,128)S(1)}, u32[]{:S(2)}, u32[]{:S(2)}) async-start(f32[8,1,64]{2,1,0:T(1,128)} %broadcast_in_dim.32), calls=%async_computation.1 | async-start | bytes 8192 | tf_op jit(solution)/shard_map/all_to_all | solution.py:40
  154.9 4.9 %all-to-all-done = f32[8,1,64]{2,1,0:T(1,128)S(1)} async-done(((f32[8,1,64]{2,1,0:T(1,128)}), f32[8,1,64]{2,1,0:T(1,128)S(1)}, u32[]{:S(2)}, u32[]{:S(2)}) %all-to-all-start) | async-done | bytes 2080 | tf_op jit(solution)/shard_map/all_to_all | solution.py:40
  159.9 0.5 broadcast_multiply_fusion
  160.4 60.4 %reduce-scatter.2.cloned.1.call-done = f32[320,512]{1,0:T(8,128)} async-done(((f32[320,4096]{1,0:T(8,128)}), f32[320,512]{1,0:T(8,128)}) %reduce-scatter.2.cloned.1.call-update) | async-done | bytes 655376 | tf_op jit(solution)/shard_map/reduce_scatter | solution.py:34
  220.8 1.9 fusion
  222.7 1.6 fusion.2
  (4 shorter events, 0.0 us)
Async XLA Ops:
  7.2 1.1 copy-start
  7.2 84.1 %all-gather.3.cloned.1.call-start = ((), (), s32[]{:S(2)}) async-start(), calls=%async_computation.2 | async-start | bytes 4456448 | tf_op jit(solution)/shard_map/all_gather | solution.py:20
  15.9 114.4 %all-gather.5.cloned.1.call-start = ((), (), s32[]{:S(2)}) async-start(), calls=%async_computation.3 | async-start | bytes 12582912 | tf_op jit(solution)/shard_map/all_gather | solution.py:20
  91.3 129.6 %reduce-scatter.2.cloned.1.call-start = ((), (), s32[]{:S(2)}) async-start(), calls=%async_computation.4 | async-start | bytes 5898240 | tf_op jit(solution)/shard_map/reduce_scatter | solution.py:34
  138.7 6.2 %copy-start.1 = (bf16[16,2,2,64,1024]{4,3,2,1,0:T(8,128)(2,1)S(1)}, bf16[16,2,2,64,1024]{4,3,2,1,0:T(8,128)(2,1)}, u32[]{:S(2)}) copy-start(bf16[16,2,2,64,1024]{4,3,2,1,0:T(8,128)(2,1)} %copy.8) | copy-start | bytes 25165828
  151.0 8.9 %all-to-all-start = ((f32[8,1,64]{2,1,0:T(1,128)}), f32[8,1,64]{2,1,0:T(1,128)S(1)}, u32[]{:S(2)}, u32[]{:S(2)}) async-start(f32[8,1,64]{2,1,0:T(1,128)} %broadcast_in_dim.32), calls=%async_computation.1 | async-start | bytes 8192 | tf_op jit(solution)/shard_map/all_to_all | solution.py:40
Sparse Core Ops, SparseCore 0:
  16.0 75.1 all-gather.2
  93.3 36.9 all-gather.4
  150.3 70.4 reduce-scatter.1
where the time goes:
time: 231 us
  waiting for transfers between devices  180 us (78%)
  between operations  13.8 us (6%)
  local copies, waits for them, and re-layouts  9.99 us (4%)
  matrix products  8.59 us (4%)
  other arithmetic  7.93 us (3%)
  blocking collectives  6.85 us (3%)
  starting transfers between devices  4.01 us (2%)
    all_gather x2, waiting for transfers between devices, all_blocks(): pieces = lax.all_gather(pieces, axes[k], axis=0, tiled=True)  114 us
    reduce_scatter x1, waiting for transfers between devices, side_by_side(): whole = lax.psum_scatter(both, axis, scatter_dimension=dim, tiled=True)  60.4 us
    dot_general x2, matrix products, contract(): lax.dot_general(left, right, (((1,), (1,)), ((), ())), preferred_element_...  8.59 us
    transpose x1, local copies, waits for them, and re-layouts, all_blocks(): pieces.transpose(*turned, *range(len(turns), pieces.ndim))  8.4 us
    all_gather x1, blocking collectives, all_blocks(): pieces = lax.all_gather(pieces, axes[k], axis=0, tiled=True)  6.85 us
    all_to_all x1, waiting for transfers between devices, sent_to_all(): return lax.all_to_all(copies, axis, split_axis=0, concat_axis=0, tiled=True)  4.94 us
  transfers between devices with their start and end apart: 4, of which 4 were waited for; matrix products, arithmetic and copies ran while one was open for 1% of the time, Pallas kernels for 0%

commit v1 on v0

--- a/solution.py
+++ b/solution.py
@@ -17,7 +17,8 @@
 def all_blocks(value, axes, turns):
     pieces = value[None]
     for k in turns:
-        pieces = lax.all_gather(pieces, axes[k], axis=0, tiled=True)
+        repeated = jnp.stack([pieces] * lax.axis_size(axes[k]))
+        pieces = jnp.concatenate(lax.all_to_all(repeated, axes[k], 0, 0), axis=0)
     current = [lax.axis_size(axes[k]) for k in reversed(turns)]
     pieces = pieces.reshape(*current, *value.shape)
     turned = sorted(range(len(turns)), key=lambda place: turns[len(turns) - 1 - place])

time: 231 us -> 339 us (1.47)
  blocking collectives: 6.85 us -> 230 us
  waiting for transfers between devices: 180 us -> 59.1 us
  other arithmetic: 7.93 us -> 11.9 us
    all_to_all x0 -> x3, blocking collectives: none -> 230 us  [all_blocks(): pieces = jnp.concatenate(lax.all_to_all(repeated, axes[k], 0, 0), axis=0)]
    all_gather x2 -> x0, waiting for transfers between devices: 114 us -> none  [all_blocks(): pieces = lax.all_gather(pieces, axes[k], axis=0, tiled=True)]
    transpose x1 -> x0, local copies, waits for them, and re-layouts: 8.4 us -> none  [all_blocks(): pieces.transpose(*turned, *range(len(turns), pieces.ndim))]
    all_to_all x0 -> x1, local copies, waits for them, and re-layouts: none -> 8.39 us  [all_blocks(): pieces = jnp.concatenate(lax.all_to_all(repeated, axes[k], 0, 0), axis=0)]
    all_gather x1 -> x0, blocking collectives: 6.85 us -> none  [all_blocks(): pieces = lax.all_gather(pieces, axes[k], axis=0, tiled=True)]
    reduce_scatter x1, waiting for transfers between devices: 60.4 us -> 54.1 us  [side_by_side(): whole = lax.psum_scatter(both, axis, scatter_dimension=dim, tiled=True)]
    another operation x0 -> x2, other arithmetic: none -> 3.95 us  [all_blocks(): repeated = jnp.stack([pieces] * lax.axis_size(axes[k]))]
  transfers between devices with their start and end apart: 4 -> 2, of which waited for: 4 -> 2; matrix products, arithmetic and copies ran while one was open for 1% -> 0% of each run, Pallas kernels for 0% -> 0%
where the time goes in v1:
time: 339 us; the launch traced here: 338 us
  blocking collectives  230 us (68%)
  waiting for transfers between devices  59.1 us (17%)
  between operations  14.1 us (4%)
  other arithmetic  11.9 us (4%)
  local copies, waits for them, and re-layouts  10.5 us (3%)
  matrix products  8.6 us (3%)
  starting transfers between devices  4.17 us (1%)
    all_to_all x3, blocking collectives, all_blocks(): pieces = jnp.concatenate(lax.all_to_all(repeated, axes[k], 0, 0), axis=0)  230 us
    reduce_scatter x1, waiting for transfers between devices, side_by_side(): whole = lax.psum_scatter(both, axis, scatter_dimension=dim, tiled=True)  54.1 us
    dot_general x2, matrix products, contract(): lax.dot_general(left, right, (((1,), (1,)), ((), ())), preferred_element_...  8.6 us
    all_to_all x1, local copies, waits for them, and re-layouts, all_blocks(): pieces = jnp.concatenate(lax.all_to_all(repeated, axes[k], 0, 0), axis=0)  8.39 us
  transfers between devices with their start and end apart: 2, of which 2 were waited for; matrix products, arithmetic and copies ran while one was open for 0% of the time, Pallas kernels for 0%

profile of v1, /device:TPU:1, one launch (start us, length us, event | category | flops | bytes accessed | tf_op | source)
XLA Modules:
  0.0 338.0 jit_solution(697026133427491118)
XLA Ops:
  7.2 0.0 copy-start
  7.2 0.0 reduce-scatter.2.cloned.1.call-start
  7.2 0.7 compare_and_fusion
  8.0 0.3 copy-done
  8.2 0.7 gather_fusion
  8.9 0.1 bitcast_select_fusion
  9.0 10.3 %all_to_all.21 = bf16[2,1,64,1024]{3,2,1,0:T(8,128)(2,1)S(1)} all-to-all(bf16[2,1,64,1024]{3,2,1,0:T(8,128)(2,1)S(1)} %pad_maximum_fusion.2), channel_id=1, replica_groups=mesh['grid_0'=16,'grid_1'=2,'grid_2'=2,'orb'=8] {'grid_1'}, dimensions={0} | all-to-all | bytes 524288 | tf_op jit(solution)/shard_map/all_to_all | solution.py:21
  19.4 0.5 stack.10
  19.9 194.1 %all_to_all.22 = bf16[16,2,64,1024]{3,2,1,0:T(8,128)(2,1)S(1)} all-to-all(bf16[16,2,64,1024]{3,2,1,0:T(8,128)(2,1)S(1)} %stack.10), channel_id=1, replica_groups=mesh['grid_0'=16,'grid_1'=2,'grid_2'=2,'orb'=8] {'grid_0'}, dimensions={0} | all-to-all | bytes 8388608 | tf_op jit(solution)/shard_map/all_to_all | solution.py:21
  214.0 3.9 %pad_maximum_fusion = bf16[2,32,64,1024]{3,2,1,0:T(8,128)(2,1)} fusion(bf16[1,32,64,1024]{3,2,1,0:T(8,128)(2,1)S(1)} %bitcast.17), kind=kLoop, calls=%fused_computation.1 | loop fusion | flops 4194304 | bytes 12582912 | tf_op jit(solution)/shard_map/stack | solution.py:20
  217.9 25.2 %all_to_all.23 = bf16[2,32,64,1024]{3,2,1,0:T(8,128)(2,1)} all-to-all(bf16[2,32,64,1024]{3,2,1,0:T(8,128)(2,1)} %pad_maximum_fusion), channel_id=1, replica_groups=mesh['grid_0'=16,'grid_1'=2,'grid_2'=2,'orb'=8] {'grid_2'}, dimensions={0} | all-to-all | bytes 16777216 | tf_op jit(solution)/shard_map/all_to_all | solution.py:21
  243.1 8.4 %copy.7 = bf16[2,32,64,1024]{3,2,0,1:T(8,128)(2,1)} copy(bf16[2,32,64,1024]{3,2,1,0:T(8,128)(2,1)} %all_to_all.23) | data formatting | bytes 16777216 | tf_op jit(solution)/shard_map/all_to_all | solution.py:21
  251.5 0.0 copy-start.1
  251.5 6.2 %fusion.3 = f32[64,4096]{1,0:T(8,128)S(1)} fusion(bf16[4096,1024]{1,0:T(8,128)(2,1)} %bitcast.15, bf16[64,1024]{1,0:T(8,128)(2,1)S(1)} %gather_fusion, pred[64]{0:T(512)(128)(4,1)S(1)} %get-tuple-element.3), kind=kOutput, calls=%fused_computation.13 | convolution fusion | flops 536936448 | bytes 9568320 | tf_op jit(solution)/shard_map/dot_general | solution.py:49
  257.7 0.0 copy-done.1
  257.8 2.4 convolution_bitcast_fusion
  260.2 2.9 pad_maximum_fusion.1
  263.0 0.0 reduce-scatter.2.cloned.1.call-update
  263.1 0.2 multiply_reduce_fusion
  263.3 0.6 broadcast_in_dim.31
  263.9 4.1 %all-to-all-start.3 = ((f32[8,1,64]{2,1,0:T(1,128)}), f32[8,1,64]{2,1,0:T(1,128)S(1)}, u32[]{:S(2)}, u32[]{:S(2)}) async-start(f32[8,1,64]{2,1,0:T(1,128)} %broadcast_in_dim.31), calls=%async_computation.4 | async-start | bytes 8192 | tf_op jit(solution)/shard_map/all_to_all | solution.py:41
  268.0 4.9 %all-to-all-done.3 = f32[8,1,64]{2,1,0:T(1,128)S(1)} async-done(((f32[8,1,64]{2,1,0:T(1,128)}), f32[8,1,64]{2,1,0:T(1,128)S(1)}, u32[]{:S(2)}, u32[]{:S(2)}) %all-to-all-start.3) | async-done | bytes 2080 | tf_op jit(solution)/shard_map/all_to_all | solution.py:41
  273.0 0.5 broadcast_multiply_fusion
  273.5 54.1 %reduce-scatter.2.cloned.1.call-done = f32[320,512]{1,0:T(8,128)} async-done(((f32[320,4096]{1,0:T(8,128)}), f32[320,512]{1,0:T(8,128)}) %reduce-scatter.2.cloned.1.call-update) | async-done | bytes 655376 | tf_op jit(solution)/shard_map/reduce_scatter | solution.py:35
  327.6 1.9 fusion
  329.5 1.6 fusion.2
  (5 shorter events, 0.1 us)
Async XLA Ops:
  7.2 1.1 copy-start
  7.2 320.4 %reduce-scatter.2.cloned.1.call-start = ((), (), s32[]{:S(2)}) async-start(), calls=%async_computation.5 | async-start | bytes 5898240 | tf_op jit(solution)/shard_map/reduce_scatter | solution.py:35
  251.5 6.2 %copy-start.1 = (bf16[2,32,64,1024]{3,2,0,1:T(8,128)(2,1)S(1)}, bf16[2,32,64,1024]{3,2,0,1:T(8,128)(2,1)}, u32[]{:S(2)}) copy-start(bf16[2,32,64,1024]{3,2,0,1:T(8,128)(2,1)} %copy.7) | copy-start | bytes 25165828
  263.9 9.1 %all-to-all-start.3 = ((f32[8,1,64]{2,1,0:T(1,128)}), f32[8,1,64]{2,1,0:T(1,128)S(1)}, u32[]{:S(2)}, u32[]{:S(2)}) async-start(f32[8,1,64]{2,1,0:T(1,128)} %broadcast_in_dim.31), calls=%async_computation.4 | async-start | bytes 8192 | tf_op jit(solution)/shard_map/all_to_all | solution.py:41
Sparse Core Ops, SparseCore 0:
  263.2 64.3 reduce-scatter.1
